TPU v7x, 32 devices: a whole 2x2x4 slice. The times are simulated.
32 devices in a mesh: rep: 8 (over y, x, core), fsdp: 4 (over z).
Axes of the slice: x: 2, y: 2, z: 4, core: 2. Of those that a mesh axis runs over, the one named last changes fastest.
Arguments:
- tokens: bfloat16 [4096, 4096], P('rep', 'fsdp'), may hold values from -6 to 6
- gate_weight: bfloat16 [4096, 7168], P('rep', 'fsdp'), may hold values from -0.09375 to 0.09375
- up_act: bfloat16 [4096, 7168], P('rep', 'fsdp'), may hold values from -6 to 6
- cotangent: bfloat16 [4096, 7168], P('rep', 'fsdp'), may hold values from -0.099609375 to 0.099609375
Outputs:
- grad_sum: bfloat16 [4096, 7168], P('rep', 'fsdp')
- curvature: float32 [7168], P('fsdp')
- spread: float32 [7168], P('fsdp')
All inputs are finite; a program needn't handle non-finite values.
Results may differ from a plain program's by a relative error of at most 0.024.
Values may be sent and summed in bfloat16 or wider, within the bound.
A program may use at most 128 MiB of HBM per device.

v0:
```python
import jax
import jax.numpy as jnp
from jax import lax
from jax.sharding import PartitionSpec as P


def shards(tokens, gate_weight, up_act, cotangent):
    features_all = lax.all_gather(tokens, "fsdp", axis=1, tiled=True)
    replicas = lax.axis_size("rep")

    def add_rows(block_rows):
        return jnp.dot(features_all, block_rows, preferred_element_type=jnp.float32)

    gate_pre = add_rows(lax.all_gather(gate_weight, "rep", axis=0, tiled=True))
    sigmoid_gate = jax.nn.sigmoid(gate_pre)
    deriv_one = sigmoid_gate * (1.0 + gate_pre * (1.0 - sigmoid_gate))
    deriv_two = sigmoid_gate * (1.0 - sigmoid_gate) * (2.0 + gate_pre * (1.0 - 2.0 * sigmoid_gate))
    weighted = cotangent.astype(jnp.float32) * up_act.astype(jnp.float32)
    token_coeff = (weighted * deriv_one).astype(jnp.bfloat16)
    bend_weight = weighted * deriv_two
    rep_grad = lax.dot_general(
        features_all, token_coeff, (((0,), (0,)), ((), ())), preferred_element_type=jnp.float32
    ).astype(jnp.bfloat16)
    own_proj = jnp.dot(features_all, rep_grad, preferred_element_type=jnp.float32)
    grad_shard = lax.psum_scatter(
        rep_grad.astype(jnp.float32).astype(jnp.bfloat16), "rep", scatter_dimension=0, tiled=True
    )
    mean_proj = add_rows(lax.all_gather(grad_shard, "rep", axis=0, tiled=True)) / replicas
    deviate = own_proj - mean_proj
    curv_part = jnp.sum(bend_weight * mean_proj * mean_proj, axis=0)
    spread_part = jnp.sum(bend_weight * deviate * deviate, axis=0)
    curvature, spread_total = lax.psum((curv_part, spread_part), "rep")
    return (grad_shard, curvature, spread_total / (replicas - 1))


def solution(mesh):
    placed = (P("rep", "fsdp"), P("rep", "fsdp"), P("rep", "fsdp"), P("rep", "fsdp"))
    return jax.shard_map(
        shards,
        mesh=mesh,
        in_specs=placed,
        out_specs=(P("rep", "fsdp"), P("fsdp"), P("fsdp")),
        check_vma=False,
    )
```

profile of v0, /device:TPU:0, one launch (start us, length us, event | category | flops | bytes accessed | tf_op | source)
XLA Modules:
  0.0 455.3 jit_solution(8435540799089013819)
XLA Ops:
  7.2 0.0 all-gather.4.cloned.1.call-start
  7.2 0.7 all-gather.4.cloned.1.call-update
  7.9 0.0 all-gather.6.cloned.1.call-start
  7.9 0.7 all-gather.6.cloned.1.call-update
  8.6 0.0 copy-start.2
  8.7 0.0 reduce-scatter.2.cloned.1.call-start
  8.7 84.3 %all-gather.4.cloned.1.call-done = bf16[512,4096]{1,0:T(8,128)(2,1)} async-done(((bf16[512,1024]{1,0:T(8,128)(2,1)}), bf16[512,4096]{1,0:T(8,128)(2,1)}) %all-gather.4.cloned.1.call-update) | async-done | bytes 4194320 | tf_op jit(solution)/shard_map/all_gather | solution.py:8
  93.0 81.3 %all-gather.6.cloned.1.call-done = bf16[4096,1792]{1,0:T(8,128)(2,1)} async-done(((bf16[512,1792]{1,0:T(8,128)(2,1)}), bf16[4096,1792]{1,0:T(8,128)(2,1)}) %all-gather.6.cloned.1.call-update) | async-done | bytes 14680080 | tf_op jit(solution)/shard_map/all_gather | solution.py:14
  174.3 0.0 copy-start
  174.3 0.0 copy-start.3
  174.3 16.7 %fusion.11 = f32[512,1792]{1,0:T(8,128)} fusion(bf16[512,4096]{1,0:T(8,128)(2,1)} %all-gather.4.cloned.1.call-done, bf16[4096,1792]{1,0:T(8,128)(2,1)} %all-gather.6.cloned.1.call-done), kind=kOutput, calls=%fused_computation.20 | convolution fusion | flops 7516192768 | bytes 22544384 | tf_op jit(solution)/shard_map/dot_general | solution.py:12
  191.0 0.0 copy-done.2
  191.0 0.0 copy-done
  191.0 0.0 copy-done.3
  191.0 15.3 %convolution_convert_fusion = bf16[1792,4096]{1,0:T(8,128)(2,1)} fusion(bf16[512,4096]{1,0:T(8,128)(2,1)S(1)} %copy-done, f32[512,1792]{1,0:T(8,128)} %fusion.11, bf16[512,1792]{1,0:T(8,128)(2,1)S(1)} %copy-done.2, bf16[512,1792]{1,0:T(8,128)(2,1)S(1)} %copy-done.3), kind=kOutput, calls=%fused_computation | convolution fusion | flops 7534542848 | bytes 26214400 | tf_op jit(solution)/shard_map/dot_general | solution.py:21
  206.3 0.0 reduce-scatter.2.cloned.1.call-update
  206.4 0.2 all-gather.8.cloned.1.call-start
  206.6 102.2 %reduce-scatter.2.cloned.1.call-done = bf16[512,1792]{0,1:T(8,128)(2,1)} async-done(((bf16[4096,1792]{0,1:T(8,128)(2,1)}), bf16[512,1792]{0,1:T(8,128)(2,1)}) %reduce-scatter.2.cloned.1.call-update) | async-done | bytes 1835024 | tf_op jit(solution)/shard_map/reduce_scatter | solution.py:25
  308.8 0.0 all-gather.8.cloned.1.call-update
  308.8 3.8 copy.7
  312.6 81.6 %all-gather.8.cloned.1.call-done = bf16[4096,1792]{0,1:T(8,128)(2,1)} async-done(((bf16[512,1792]{0,1:T(8,128)(2,1)}), bf16[4096,1792]{0,1:T(8,128)(2,1)}) %all-gather.8.cloned.1.call-update) | async-done | bytes 14680080 | tf_op jit(solution)/shard_map/all_gather | solution.py:28
  394.2 0.0 copy-start.1
  394.2 0.0 copy-start.4
  394.2 0.0 copy-start.5
  394.2 16.5 %fusion.6 = (f32[1792]{0:T(1024)S(1)}, f32[1792,512]{0,1:T(8,128)S(1)}) fusion(f32[512,1792]{1,0:T(8,128)} %fusion.11, bf16[512,1792]{1,0:T(8,128)(2,1)S(1)} %copy-done.2, bf16[512,1792]{1,0:T(8,128)(2,1)} %param.7, bf16[4096,1792]{0,1:T(8,128)(2,1)} %all-gather.8.cloned.1.call-done, bf16[512,4096]{1,0:T(8,128)(2,1)} %all-gather.4.cloned.1.call-done), kind=kOutput, calls=%fused_computation.11 | convolution fusion | flops 7532705792 | bytes 29891584 | tf_op jit(solution)/shard_map/dot_general | solution.py:12
  410.8 0.0 copy-done.1
  410.8 0.0 copy-done.4
  410.8 0.0 copy-done.5
  410.8 13.8 %fusion.7 = f32[1792]{0:T(1024)S(1)} fusion(f32[1792,512]{0,1:T(8,128)S(1)} %get-tuple-element.9, bf16[1792,4096]{1,0:T(8,128)(2,1)} %convolution_convert_fusion, bf16[512,4096]{1,0:T(8,128)(2,1)S(1)} %copy-done.1, f32[512,1792]{1,0:T(8,128)S(1)} %copy-done.5, bf16[512,1792]{1,0:T(8,128)(2,1)S(1)} %copy-done.2, bf16[512,1792]{1,0:T(8,128)(2,1)S(1)} %copy-done.4), kind=kOutput, calls=%fused_computation.12 | convolution fusion | flops 7532705792 | bytes 29891584 | tf_op jit(solution)/shard_map/dot_general | solution.py:24
  424.7 23.5 %all-reduce = (f32[1792]{0:T(1024)}, f32[1792]{0:T(1024)S(1)}) all-reduce(f32[1792]{0:T(1024)S(1)} %get-tuple-element.8, f32[1792]{0:T(1024)S(1)} %fusion.7), channel_id=1, replica_groups=mesh['rep'=8,'fsdp'=4] {'rep'}, use_global_device_ids=true, to_apply=%region_2.0 | all-reduce | flops 3584 | bytes 28672 | tf_op jit(solution)/shard_map/psum | solution.py:32
  448.1 0.6 broadcast_multiply_fusion
Async XLA Ops:
  7.2 85.9 %all-gather.4.cloned.1.call-start = ((), (), s32[]{:S(2)}) async-start(), calls=%async_computation.1 | async-start | bytes 5242880 | tf_op jit(solution)/shard_map/all_gather | solution.py:8
  7.9 166.4 %all-gather.6.cloned.1.call-start = ((), (), s32[]{:S(2)}) async-start(), calls=%async_computation.2 | async-start | bytes 16515072 | tf_op jit(solution)/shard_map/all_gather | solution.py:14
  8.6 182.4 %copy-start.2 = (bf16[512,1792]{1,0:T(8,128)(2,1)S(1)}, bf16[512,1792]{1,0:T(8,128)(2,1)}, u32[]{:S(2)}) copy-start(bf16[512,1792]{1,0:T(8,128)(2,1)} %param.6) | copy-start | bytes 5505028
  8.7 300.1 %reduce-scatter.2.cloned.1.call-start = ((), (), s32[]{:S(2)}) async-start(), calls=%async_computation.3 | async-start | bytes 16515072 | tf_op jit(solution)/shard_map/reduce_scatter | solution.py:25
  174.3 16.7 %copy-start = (bf16[512,4096]{1,0:T(8,128)(2,1)S(1)}, bf16[512,4096]{1,0:T(8,128)(2,1)}, u32[]{:S(2)}) copy-start(bf16[512,4096]{1,0:T(8,128)(2,1)} %all-gather.4.cloned.1.call-done) | copy-start | bytes 12582916
  174.3 16.7 %copy-start.3 = (bf16[512,1792]{1,0:T(8,128)(2,1)S(1)}, bf16[512,1792]{1,0:T(8,128)(2,1)}, u32[]{:S(2)}) copy-start(bf16[512,1792]{1,0:T(8,128)(2,1)} %param.7) | copy-start | bytes 5505028
  206.4 187.9 %all-gather.8.cloned.1.call-start = ((), (), s32[]{:S(2)}) async-start(), calls=%async_computation.4 | async-start | bytes 16515072 | tf_op jit(solution)/shard_map/all_gather | solution.py:28
  394.2 16.5 %copy-start.1 = (bf16[512,4096]{1,0:T(8,128)(2,1)S(1)}, bf16[512,4096]{1,0:T(8,128)(2,1)}, u32[]{:S(2)}) copy-start(bf16[512,4096]{1,0:T(8,128)(2,1)} %all-gather.4.cloned.1.call-done) | copy-start | bytes 12582916
  394.2 16.6 %copy-start.4 = (bf16[512,1792]{1,0:T(8,128)(2,1)S(1)}, bf16[512,1792]{1,0:T(8,128)(2,1)}, u32[]{:S(2)}) copy-start(bf16[512,1792]{1,0:T(8,128)(2,1)} %param.7) | copy-start | bytes 5505028
  394.2 16.6 %copy-start.5 = (f32[512,1792]{1,0:T(8,128)S(1)}, f32[512,1792]{1,0:T(8,128)}, u32[]{:S(2)}) copy-start(f32[512,1792]{1,0:T(8,128)} %fusion.11) | copy-start | bytes 11010052
Sparse Core Ops, SparseCore 0:
  9.5 83.4 all-gather.3
  94.9 79.3 all-gather.5
  206.5 102.2 reduce-scatter.1
  310.5 83.7 all-gather.7
where the time goes:
time: 456 us; the launch traced here: 455 us
  waiting for transfers between devices  351 us (77%)
  matrix products  62.4 us (14%)
  blocking collectives  23.5 us (5%)
  between operations  13.8 us (3%)
    reduce_scatter x1, waiting for transfers between devices, shards(): lax.psum_scatter(rep_grad.astype(jnp.float32).astype(jnp.bfloat16), 'rep'...  102 us
    all_gather x1, waiting for transfers between devices, shards(): features_all = lax.all_gather(tokens, 'fsdp', axis=1, tiled=True)  84.3 us
    all_gather x1, waiting for transfers between devices, shards(): lax.all_gather(grad_shard, 'rep', axis=0, tiled=True)  81.6 us
    all_gather x1, waiting for transfers between devices, shards(): gate_pre = add_rows(lax.all_gather(gate_weight, 'rep', axis=0, tiled=True))  81.3 us
    dot_general x2, matrix products, add_rows(): return jnp.dot(features_all, block_rows, preferred_element_type=jnp.float32)  33.2 us
    psum x1, blocking collectives, shards(): curvature, spread_total = lax.psum((curv_part, spread_part), 'rep')  23.5 us
    dot_general x1, matrix products, shards(): lax.dot_general(features_all, token_coeff, (((0,), (0,)), ((), ())), pref...  15.3 us
    dot_general x1, matrix products, shards(): jnp.dot(features_all, rep_grad, preferred_element_type=jnp.float32)  13.8 us
  transfers between devices with their start and end apart: 4, of which 4 were waited for; matrix products, arithmetic and copies ran while one was open for 1% of the time, Pallas kernels for 0%

commit v1 on v0

--- a/solution.py
+++ b/solution.py
@@ -1,11 +1,30 @@
+import functools
 import jax
 import jax.numpy as jnp
 from jax import lax
 from jax.sharding import PartitionSpec as P
 
 
+def _test_heads(matrix, axis_key, dimension_no):
+    q_n = jax.lax.axis_size(axis_key)
+    seen_now = matrix
+    chunks = [seen_now]
+    v_next = [(it - 1, it) for it in range(1, q_n)] + [(q_n - 1, 0)]
+    for _ in [*range(q_n - 1)]:
+        seen_now = jax.lax.ppermute(seen_now, axis_key, v_next)
+        chunks += [seen_now]
+    return jnp.roll(
+        jnp.concatenate([*reversed(chunks)], axis=dimension_no),
+        (jax.lax.axis_index(axis_key) + 1) * seen_now.shape[dimension_no],
+        axis=dimension_no,
+    )
+
+
+finish_the_columns = functools.partial(_test_heads, axis_key="fsdp", dimension_no=1)
+
+
 def shards(tokens, gate_weight, up_act, cotangent):
-    features_all = lax.all_gather(tokens, "fsdp", axis=1, tiled=True)
+    features_all = finish_the_columns(tokens)
     replicas = lax.axis_size("rep")
 
     def add_rows(block_rows):

time: 456 us -> 376 us (0.82)
  waiting for transfers between devices: 351 us -> 263 us
  local copies, waits for them, and re-layouts: 3.83 us -> 13.5 us
    all_gather x1 -> x0, waiting for transfers between devices: 84.3 us -> none  [shards(): features_all = lax.all_gather(tokens, 'fsdp', axis=1, tiled=True)]
    all_gather x1, waiting for transfers between devices: 81.3 us -> 0.01 us  [shards(): gate_pre = add_rows(lax.all_gather(gate_weight, 'rep', axis=0, tiled=True))]
    ppermute x0 -> x3, waiting for transfers between devices: none -> 76.9 us  [_test_heads(): seen_now = jax.lax.ppermute(seen_now, axis_key, v_next)]
    unnamed x13 -> x19, local copies, waits for them, and re-layouts: 3.83 us -> 12.3 us
    dot_general x2, matrix products: 33.2 us -> 28.2 us  [add_rows(): return jnp.dot(features_all, block_rows, preferred_element_type=jnp.float32)]
  transfers between devices with their start and end apart: 4 -> 6, of which waited for: 4 -> 5; matrix products, arithmetic and copies ran while one was open for 1% -> 3% of each run, Pallas kernels for 0% -> 0%
where the time goes in v1:
time: 376 us
  waiting for transfers between devices  263 us (70%)
  matrix products  58 us (15%)
  blocking collectives  23.5 us (6%)
  between operations  13.8 us (4%)
  local copies, waits for them, and re-layouts  13.5 us (4%)
    reduce_scatter x1, waiting for transfers between devices, shards(): lax.psum_scatter(rep_grad.astype(jnp.float32).astype(jnp.bfloat16), 'rep'...  102 us
    all_gather x1, waiting for transfers between devices, shards(): lax.all_gather(grad_shard, 'rep', axis=0, tiled=True)  83.3 us
    ppermute x3, waiting for transfers between devices, _test_heads(): seen_now = jax.lax.ppermute(seen_now, axis_key, v_next)  76.9 us
    dot_general x2, matrix products, add_rows(): return jnp.dot(features_all, block_rows, preferred_element_type=jnp.float32)  28.2 us
    psum x1, blocking collectives, shards(): curvature, spread_total = lax.psum((curv_part, spread_part), 'rep')  23.5 us
    dot_general x1, matrix products, shards(): jnp.dot(features_all, rep_grad, preferred_element_type=jnp.float32)  15 us
    dot_general x1, matrix products, shards(): lax.dot_general(features_all, token_coeff, (((0,), (0,)), ((), ())), pref...  14.8 us
    unnamed x19, local copies, waits for them, and re-layouts  12.3 us
  transfers between devices with their start and end apart: 6, of which 5 were waited for; matrix products, arithmetic and copies ran while one was open for 3% of the time, Pallas kernels for 0%

profile of v1, /device:TPU:0, one launch (start us, length us, event | category | flops | bytes accessed | tf_op | source)
XLA Modules:
  0.0 376.0 jit_solution(3544414058344754333)
XLA Ops:
  7.2 0.0 copy-start
  7.2 0.0 all-gather.3.cloned.1.call-start
  7.2 0.7 all-gather.3.cloned.1.call-update
  7.9 0.0 reduce-scatter.2.cloned.1.call-start
  8.0 3.1 collective-permute-start
  11.1 25.4 %collective-permute-done = bf16[512,1024]{1,0:T(8,128)(2,1)S(1)} collective-permute-done((bf16[512,1024]{1,0:T(8,128)(2,1)}, bf16[512,1024]{1,0:T(8,128)(2,1)S(1)}, u32[]{:S(2)}, u32[]{:S(2)}) %collective-permute-start) | collective-permute-done | bytes 1048608 | tf_op jit(solution)/shard_map/ppermute | solution.py:14
  36.5 0.0 collective-permute-start.1
  36.5 26.1 %collective-permute-done.1 = bf16[512,1024]{1,0:T(8,128)(2,1)S(1)} collective-permute-done((bf16[512,1024]{1,0:T(8,128)(2,1)S(1)}, bf16[512,1024]{1,0:T(8,128)(2,1)S(1)}, u32[]{:S(2)}, u32[]{:S(2)}) %collective-permute-start.1) | collective-permute-done | bytes 1048608 | tf_op jit(solution)/shard_map/ppermute | solution.py:14
  62.6 0.0 collective-permute-start.2
  62.6 25.4 %collective-permute-done.2 = bf16[512,1024]{1,0:T(8,128)(2,1)} collective-permute-done((bf16[512,1024]{1,0:T(8,128)(2,1)S(1)}, bf16[512,1024]{1,0:T(8,128)(2,1)}, u32[]{:S(2)}, u32[]{:S(2)}) %collective-permute-start.2) | collective-permute-done | bytes 1048608 | tf_op jit(solution)/shard_map/ppermute | solution.py:14
  87.9 2.4 constant_dynamic-update-slice_fusion.7
  90.4 1.1 constant_dynamic-update-slice_fusion.6
  91.5 1.1 constant_dynamic-update-slice_fusion.5
  92.6 0.0 copy-done
  92.6 1.2 constant_dynamic-update-slice_fusion.4
  93.8 2.4 constant_dynamic-update-slice_fusion.3
  96.2 1.2 constant_dynamic-update-slice_fusion.2
  97.3 1.1 constant_dynamic-update-slice_fusion.1
  98.5 1.2 constant_dynamic-update-slice_fusion
  99.7 0.0 copy-start.1
  99.7 0.0 all-gather.3.cloned.1.call-done
  99.7 0.0 copy-start.2
  99.7 11.8 %fusion.12 = f32[512,1792]{1,0:T(8,128)S(1)} fusion(bf16[4096,1792]{1,0:T(8,128)(2,1)} %all-gather.3.cloned.1.call-done, bf16[512,8192]{1,0:T(8,128)(2,1)} %constant_dynamic-update-slice_fusion, s32[]{:T(128)S(6)} %select_n.14), kind=kOutput, calls=%fused_computation.19 | convolution fusion | flops 7516192768 | bytes 22544388 | tf_op jit(solution)/shard_map/dot_general | solution.py:31
  111.5 0.0 copy-start.4
  111.5 1.8 copy-done.4
  113.3 0.0 copy-done.1
  113.3 0.0 copy-done.2
  113.3 14.8 %convolution_convert_fusion = bf16[4096,1792]{1,0:T(8,128)(2,1)} fusion(bf16[512,8192]{1,0:T(8,128)(2,1)} %constant_dynamic-update-slice_fusion, s32[]{:T(128)S(6)} %select_n.14, f32[512,1792]{1,0:T(8,128)S(1)} %fusion.12, bf16[512,1792]{1,0:T(8,128)(2,1)S(1)} %copy-done.1, bf16[512,1792]{1,0:T(8,128)(2,1)S(1)} %copy-done.2), kind=kOutput, calls=%fused_computation | convolution fusion | flops 7534542848 | bytes 26214404 | tf_op jit(solution)/shard_map/dot_general | solution.py:40
  128.1 0.0 reduce-scatter.2.cloned.1.call-update
  128.1 0.2 all-gather.5.cloned.1.call-start
  128.3 102.3 %reduce-scatter.2.cloned.1.call-done = bf16[512,1792]{1,0:T(8,128)(2,1)} async-done(((bf16[4096,1792]{1,0:T(8,128)(2,1)}), bf16[512,1792]{1,0:T(8,128)(2,1)}) %reduce-scatter.2.cloned.1.call-update) | async-done | bytes 1835024 | tf_op jit(solution)/shard_map/reduce_scatter | solution.py:44
  230.6 0.0 all-gather.5.cloned.1.call-update
  230.6 83.3 %all-gather.5.cloned.1.call-done = bf16[4096,1792]{1,0:T(8,128)(2,1)} async-done(((bf16[512,1792]{1,0:T(8,128)(2,1)}), bf16[4096,1792]{1,0:T(8,128)(2,1)}) %all-gather.5.cloned.1.call-update) | async-done | bytes 14680080 | tf_op jit(solution)/shard_map/all_gather | solution.py:47
  314.0 0.0 copy-start.3
  314.0 0.0 copy-start.5
  314.0 16.3 %fusion.6 = (f32[1792]{0:T(1024)S(1)}, f32[512,1792]{1,0:T(8,128)S(1)}) fusion(f32[512,1792]{1,0:T(8,128)} %copy-done.4, bf16[512,1792]{1,0:T(8,128)(2,1)S(1)} %copy-done.1, bf16[512,1792]{1,0:T(8,128)(2,1)} %param.7, bf16[4096,1792]{1,0:T(8,128)(2,1)} %all-gather.5.cloned.1.call-done, bf16[512,8192]{1,0:T(8,128)(2,1)} %constant_dynamic-update-slice_fusion, ...), kind=kOutput, calls=%fused_computation.11 | convolution fusion | flops 7532705792 | bytes 29891588 | tf_op jit(solution)/shard_map/dot_general | solution.py:31
  330.3 0.0 copy-done.3
  330.3 0.0 copy-done.5
  330.4 15.0 %fusion.7 = f32[1792]{0:T(1024)S(1)} fusion(f32[512,1792]{1,0:T(8,128)S(1)} %get-tuple-element.6, bf16[4096,1792]{1,0:T(8,128)(2,1)} %convolution_convert_fusion, bf16[512,8192]{1,0:T(8,128)(2,1)} %constant_dynamic-update-slice_fusion, s32[]{:T(128)S(6)} %select_n.14, f32[512,1792]{1,0:T(8,128)S(1)} %copy-done.5, bf16[512,1792]{1,0:T(8,128)(2,1)S(1)} %copy-done.1, ...), kind=kOutput, calls=%fused_computation.12 | convolution fusion | flops 7533623296 | bytes 29891588 | tf_op jit(solution)/shard_map/dot_general | solution.py:43
  345.4 23.5 %all-reduce = (f32[1792]{0:T(1024)}, f32[1792]{0:T(1024)S(1)}) all-reduce(f32[1792]{0:T(1024)S(1)} %get-tuple-element.5, f32[1792]{0:T(1024)S(1)} %fusion.7), channel_id=1, replica_groups=mesh['rep'=8,'fsdp'=4] {'rep'}, use_global_device_ids=true, to_apply=%region_2.3 | all-reduce | flops 3584 | bytes 28672 | tf_op jit(solution)/shard_map/psum | solution.py:51
  368.9 0.6 broadcast_multiply_fusion
Async XLA Ops:
  7.2 85.5 %copy-start = (bf16[512,1024]{1,0:T(8,128)(2,1)S(1)}, bf16[512,1024]{1,0:T(8,128)(2,1)}, u32[]{:S(2)}) copy-start(bf16[512,1024]{1,0:T(8,128)(2,1)} %param.4) | copy-start | bytes 3145732
  7.2 92.5 %all-gather.3.cloned.1.call-start = ((), (), s32[]{:S(2)}) async-start(), calls=%async_computation.1 | async-start | bytes 16515072 | tf_op jit(solution)/shard_map/all_gather | solution.py:33
  7.9 222.7 %reduce-scatter.2.cloned.1.call-start = ((), (), s32[]{:S(2)}) async-start(), calls=%async_computation.2 | async-start | bytes 16515072 | tf_op jit(solution)/shard_map/reduce_scatter | solution.py:44
  8.0 28.5 %collective-permute-start = (bf16[512,1024]{1,0:T(8,128)(2,1)}, bf16[512,1024]{1,0:T(8,128)(2,1)S(1)}, u32[]{:S(2)}, u32[]{:S(2)}) collective-permute-start(bf16[512,1024]{1,0:T(8,128)(2,1)} %param.4), channel_id=1, source_target_pairs={{0,1},{1,2},{2,3},{3,0},{4,5},{5,6},{6,7},{7,4},{8,9},{9,10},{10,1... | collective-permute-start | bytes 3145736 | tf_op jit(solution)/shard_map/ppermute | solution.py:14
  36.5 26.1 %collective-permute-start.1 = (bf16[512,1024]{1,0:T(8,128)(2,1)S(1)}, bf16[512,1024]{1,0:T(8,128)(2,1)S(1)}, u32[]{:S(2)}, u32[]{:S(2)}) collective-permute-start(bf16[512,1024]{1,0:T(8,128)(2,1)S(1)} %collective-permute-done), channel_id=1, source_target_pairs={{0,1},{1,2},{2,3},{3,0},{4,5},{5,6},{6,7},{7,4},{8,9},{9,10},{10,1... | collective-permute-start | bytes 3145736 | tf_op jit(solution)/shard_map/ppermute | solution.py:14
  62.6 25.4 %collective-permute-start.2 = (bf16[512,1024]{1,0:T(8,128)(2,1)S(1)}, bf16[512,1024]{1,0:T(8,128)(2,1)}, u32[]{:S(2)}, u32[]{:S(2)}) collective-permute-start(bf16[512,1024]{1,0:T(8,128)(2,1)S(1)} %collective-permute-done.1), channel_id=1, source_target_pairs={{0,1},{1,2},{2,3},{3,0},{4,5},{5,6},{6,7},{7,4},{8,9},{9,10},{10,1... | collective-permute-start | bytes 3145736 | tf_op jit(solution)/shard_map/ppermute | solution.py:14
  99.7 13.6 %copy-start.1 = (bf16[512,1792]{1,0:T(8,128)(2,1)S(1)}, bf16[512,1792]{1,0:T(8,128)(2,1)}, u32[]{:S(2)}) copy-start(bf16[512,1792]{1,0:T(8,128)(2,1)} %param.6) | copy-start | bytes 5505028
  99.7 13.6 %copy-start.2 = (bf16[512,1792]{1,0:T(8,128)(2,1)S(1)}, bf16[512,1792]{1,0:T(8,128)(2,1)}, u32[]{:S(2)}) copy-start(bf16[512,1792]{1,0:T(8,128)(2,1)} %param.7) | copy-start | bytes 5505028
  111.5 1.8 copy-start.4
  128.1 185.9 %all-gather.5.cloned.1.call-start = ((), (), s32[]{:S(2)}) async-start(), calls=%async_computation.3 | async-start | bytes 16515072 | tf_op jit(solution)/shard_map/all_gather | solution.py:47
  314.0 16.4 %copy-start.3 = (bf16[512,1792]{1,0:T(8,128)(2,1)S(1)}, bf16[512,1792]{1,0:T(8,128)(2,1)}, u32[]{:S(2)}) copy-start(bf16[512,1792]{1,0:T(8,128)(2,1)} %param.7) | copy-start | bytes 5505028
  314.0 16.4 %copy-start.5 = (f32[512,1792]{1,0:T(8,128)S(1)}, f32[512,1792]{1,0:T(8,128)}, u32[]{:S(2)}) copy-start(f32[512,1792]{1,0:T(8,128)} %copy-done.4) | copy-start | bytes 11010052
Sparse Core Ops, SparseCore 0:
  9.9 83.5 all-gather.2
  128.2 102.3 reduce-scatter.1
  233.1 80.8 all-gather.4
